TPU v7x, 32 devices: a whole 2x2x4 slice. The times are simulated.
32 devices in a mesh: space: 8 (over z, x), sub: 4 (over y, core).
Axes of the slice: x: 2, y: 2, z: 4, core: 2. Of those that a mesh axis runs over, the one named last changes fastest.
Arguments:
- multipole: float32 [8192, 152], P('space'), may hold values from -6 to 6
- inherited: float32 [8192, 152], P(('space', 'sub')), may hold values from -6 to 6
- send_rows: int32 [8, 4, 384], P('space'), may hold values from 0 to 1023
- sources: int32 [8192, 316], P('space', 'sub'), may hold values from -1 to 2559, as said below
- operators: float32 [316, 152, 152], P('sub'), may hold values from -0.0546875 to 0.0546875
Outputs:
- local: float32 [8192, 152], P(('space', 'sub'))
Inputs may be any that keep to these rules, and one draw needn't show every extreme that they name: `sources`: an entry that names a ghost row names one whose sending block exists.
All inputs are finite; a program needn't handle non-finite values.
Results may differ from a plain program's by a relative error of at most 0.0003.
Values sent between devices are 32-bit elements; how exact they have to be, the bound alone decides.
A program may use at most 192 MiB of HBM per device.

v0:
```python
import math

import jax
import jax.numpy as jnp
from jax import lax
from jax.sharding import PartitionSpec as P


def passed_along(block, axis, distance):
    devices = range(lax.axis_size(axis))
    route = [(i - distance, i) for i in devices if i - distance in devices]
    return lax.ppermute(block, axis, route)


def local(multipole, inherited, send_rows, sources, operators):
    near_count = send_rows.shape[1] // 2
    width = multipole.shape[1]
    send_map = send_rows[0]
    payloads = []
    for peer_slot in range(2 * near_count):
        offset = peer_slot + 1 if peer_slot < near_count else near_count - 1 - peer_slot
        payloads.append(passed_along(multipole[send_map[peer_slot]], "space", offset))
    ghosts = jnp.stack(payloads)
    zero_row = jnp.zeros((1, width), multipole.dtype)
    lookup = jnp.concatenate([multipole, ghosts.reshape(-1, width), zero_row], axis=0)
    empty_row = lookup.shape[0] - 1
    flat_ops = operators.reshape(-1, width)
    block_rows = math.gcd(sources.shape[0], 512)
    block_count = sources.shape[0] // block_rows
    safe_index = jnp.where(sources >= 0, sources, empty_row)

    def one_block(running, index_block):
        picked = jnp.take(lookup, index_block.reshape(-1), axis=0)
        product = jnp.dot(
            picked.reshape(block_rows, -1),
            flat_ops,
            precision=lax.Precision.HIGHEST,
            preferred_element_type=jnp.float32,
        )
        return (running, product)

    _, partial_value = lax.scan(
        one_block, jnp.zeros((), jnp.float32), safe_index.reshape(block_count, block_rows, -1)
    )
    partial_value = partial_value.reshape(-1, width)
    summed = lax.psum_scatter(partial_value, "sub", scatter_dimension=0, tiled=True)
    return summed + inherited


def solution(mesh):
    return jax.shard_map(
        local,
        mesh=mesh,
        in_specs=(
            P("space", None),
            P(("space", "sub"), None),
            P("space", None, None),
            P("space", "sub"),
            P("sub", None, None),
        ),
        out_specs=P(("space", "sub"), None),
        check_vma=False,
    )
```

profile of v0, /device:TPU:0, one launch (start us, length us, event | category | flops | bytes accessed | tf_op | source)
XLA Modules:
  0.0 474.4 jit_solution(11779410788782126596)
XLA Ops:
  6.5 1.4 copy.38
  8.0 0.9 fusion.8
  8.9 1.7 gather_fusion.4
  10.6 1.3 collective-permute-start.3
  11.9 1.7 gather_fusion.1
  13.6 4.9 %collective-permute-start = (f32[384,152]{1,0:T(8,128)S(1)}, f32[384,152]{1,0:T(8,128)S(1)}, u32[]{:S(2)}, u32[]{:S(2)}) collective-permute-start(f32[384,152]{1,0:T(8,128)S(1)} %gather_fusion.1), channel_id=1, source_target_pairs={{0,4},{4,8},{8,12},{12,16},{16,20},{20,24},{24,28},{1,5},{5,9},{9,... | collective-permute-start | bytes 700424 | tf_op jit(solution)/shard_map/ppermute | solution.py:12
  18.5 1.7 gather_fusion.2
  20.1 4.6 collective-permute-start.1
  24.7 2.2 gather_fusion.3
  26.9 1.3 collective-permute-start.2
  28.2 15.3 %copy.39 = f32[79,152,152]{2,1,0:T(8,128)} copy(f32[79,152,152]{0,2,1:T(8,128)} %param.11) | data formatting | bytes 14601728 | tf_op args[4]
  43.5 1.0 reshape.177
  44.5 1.1 pad_maximum_fusion
  45.6 1.6 maximum_maximum_fusion
  47.3 392.8 %while.10 = (s32[]{:T(128)}, f32[2,512,152]{1,0,2:T(2,128)}, s32[2,512,79]{1,0,2:T(2,128)}, f32[2561,152]{1,0:T(8,128)S(1)}, f32[12008,152]{1,0:T(8,128)}, /*index=5*/s32[]{:T(128)}, s32[]{:T(128)}) while((s32[]{:T(128)}, f32[2,512,152]{1,0,2:T(2,128)}, s32[2,512,79]{1,0,2:T(2,128)}, f32[2561,152]{1,0:T(8,128)S(1)}, f32[12008,152]{1,0:T(8,128)}, ...), condition=%wide.region_1.2_spmd, body=%wide.region_0.1_spmd.sunk | while | flops 11220680704 | bytes 195324752 | solution.py:42
  47.5 1.1 constant_dynamic-slice_fusion.2
  49.7 95.1 %gather_fusion = f32[40448,152]{1,0:T(8,128)} fusion(f32[2561,152]{1,0:T(8,128)S(1)} %get-tuple-element.100, s32[40960]{0:T(1024)S(1)} %pad_clamp_fusion.6), kind=kCustom, calls=%fused_computation.clone.1 | custom fusion | bytes 49346560 | tf_op jit(solution)/shard_map/while/body/eval_jaxpr/jit(_take)/gather | solution.py:33
  144.8 32.8 %gather.35 = f32[512,12008]{1,0:T(8,128)} reshape(f32[40448,152]{1,0:T(8,128)} %gather_fusion) | data formatting | bytes 49184768 | tf_op jit(solution)/shard_map/while/body/eval_jaxpr/jit(_take)/gather | solution.py:33
  177.5 24.6 %copy.58 = f32[512,12008]{0,1:T(8,128)} copy(f32[512,12008]{1,0:T(8,128)} %gather.35) | data formatting | bytes 49184768 | tf_op jit(solution)/shard_map/while/body/eval_jaxpr/jit(_take)/gather | solution.py:33
  202.1 1.6 broadcast_in_dim.43
  203.7 33.0 %fusion.20 = f32[1,512,152]{1,2,0:T(8,128)S(1)} fusion(f32[12008,152]{1,0:T(8,128)} %get-tuple-element.101, pred[512,12008]{0,1:T(8,128)(4,1)S(1)} %bitcast.39, f32[512,12008]{0,1:T(8,128)} %copy.58), kind=kOutput, calls=%fused_computation.8.clone.1 | convolution fusion | flops 11220275200 | bytes 38352640 | tf_op jit(solution)/shard_map/while/body/eval_jaxpr/dot_general | solution.py:34
  237.0 6.8 %dynamic_update_slice.5 = f32[2,512,152]{1,0,2:T(2,128)} dynamic-update-slice(f32[2,512,152]{1,0,2:T(2,128)} %get-tuple-element.91, f32[1,512,152]{1,0,2:T(1,128)S(1)} %copy.59, s32[]{:T(128)} %get-tuple-element.90, s32[]{:T(128)} %constant.14.clone.1..sunk, s32[]{:T(128)} %constant.14.clone.1..sunk) | dynamic-update-slice | bytes 622596 | tf_op jit(solution)/shard_map/while/body/jit(dynamic_update_index_in_dim)/dynamic_update_slice | solution.py:42
  243.8 1.1 constant_dynamic-slice_fusion.2
  246.0 95.1 %gather_fusion = f32[40448,152]{1,0:T(8,128)} fusion(f32[2561,152]{1,0:T(8,128)S(1)} %get-tuple-element.100, s32[40960]{0:T(1024)S(1)} %pad_clamp_fusion.6), kind=kCustom, calls=%fused_computation.clone.1 | custom fusion | bytes 49346560 | tf_op jit(solution)/shard_map/while/body/eval_jaxpr/jit(_take)/gather | solution.py:33
  341.0 32.8 %gather.35 = f32[512,12008]{1,0:T(8,128)} reshape(f32[40448,152]{1,0:T(8,128)} %gather_fusion) | data formatting | bytes 49184768 | tf_op jit(solution)/shard_map/while/body/eval_jaxpr/jit(_take)/gather | solution.py:33
  373.8 24.6 %copy.58 = f32[512,12008]{0,1:T(8,128)} copy(f32[512,12008]{1,0:T(8,128)} %gather.35) | data formatting | bytes 49184768 | tf_op jit(solution)/shard_map/while/body/eval_jaxpr/jit(_take)/gather | solution.py:33
  398.4 1.6 broadcast_in_dim.43
  400.0 33.0 %fusion.20 = f32[1,512,152]{1,2,0:T(8,128)S(1)} fusion(f32[12008,152]{1,0:T(8,128)} %get-tuple-element.101, pred[512,12008]{0,1:T(8,128)(4,1)S(1)} %bitcast.39, f32[512,12008]{0,1:T(8,128)} %copy.58), kind=kOutput, calls=%fused_computation.8.clone.1 | convolution fusion | flops 11220275200 | bytes 38352640 | tf_op jit(solution)/shard_map/while/body/eval_jaxpr/dot_general | solution.py:34
  433.3 6.8 %dynamic_update_slice.5 = f32[2,512,152]{1,0,2:T(2,128)} dynamic-update-slice(f32[2,512,152]{1,0,2:T(2,128)} %get-tuple-element.91, f32[1,512,152]{1,0,2:T(1,128)S(1)} %copy.59, s32[]{:T(128)} %get-tuple-element.90, s32[]{:T(128)} %constant.14.clone.1..sunk, s32[]{:T(128)} %constant.14.clone.1..sunk) | dynamic-update-slice | bytes 622596 | tf_op jit(solution)/shard_map/while/body/jit(dynamic_update_index_in_dim)/dynamic_update_slice | solution.py:42
  440.1 2.0 copy.46
  442.1 23.8 %reduce-scatter.2.cloned.1.call-done = f32[256,152]{0,1:T(8,128)} async-done(((f32[1024,152]{0,1:T(8,128)}), f32[256,152]{0,1:T(8,128)}) %reduce-scatter.2.cloned.1.call-update) | async-done | bytes 155664 | tf_op jit(solution)/shard_map/reduce_scatter | solution.py:46
  465.9 1.6 add.74
  (31 shorter events, 2.9 us)
Async XLA Ops:
  6.5 459.4 %reduce-scatter.2.cloned.1.call-start = ((), (), s32[]{:S(2)}) async-start(), calls=%async_computation.1 | async-start | bytes 778240 | tf_op jit(solution)/shard_map/reduce_scatter | solution.py:46
  8.0 18.9 %copy-start = (f32[1024,152]{1,0:T(8,128)}, f32[1024,152]{1,0:T(8,128)S(1)}, u32[]{:S(2)}) copy-start(f32[1024,152]{1,0:T(8,128)S(1)} %copy.38) | copy-start | bytes 1867780
  10.6 33.9 %collective-permute-start.3 = (f32[384,152]{1,0:T(8,128)S(1)}, f32[384,152]{1,0:T(8,128)S(1)}, u32[]{:S(2)}, u32[]{:S(2)}) collective-permute-start(f32[384,152]{1,0:T(8,128)S(1)} %gather_fusion.4), channel_id=1, source_target_pairs={{8,0},{12,4},{16,8},{20,12},{24,16},{28,20},{9,1},{13,5},{17,9},{2... | collective-permute-start | bytes 700424 | tf_op jit(solution)/shard_map/ppermute | solution.py:12
  13.6 31.0 %collective-permute-start = (f32[384,152]{1,0:T(8,128)S(1)}, f32[384,152]{1,0:T(8,128)S(1)}, u32[]{:S(2)}, u32[]{:S(2)}) collective-permute-start(f32[384,152]{1,0:T(8,128)S(1)} %gather_fusion.1), channel_id=1, source_target_pairs={{0,4},{4,8},{8,12},{12,16},{16,20},{20,24},{24,28},{1,5},{5,9},{9,... | collective-permute-start | bytes 700424 | tf_op jit(solution)/shard_map/ppermute | solution.py:12
  20.1 24.4 %collective-permute-start.1 = (f32[384,152]{1,0:T(8,128)S(1)}, f32[384,152]{1,0:T(8,128)S(1)}, u32[]{:S(2)}, u32[]{:S(2)}) collective-permute-start(f32[384,152]{1,0:T(8,128)S(1)} %gather_fusion.2), channel_id=1, source_target_pairs={{0,8},{4,12},{8,16},{12,20},{16,24},{20,28},{1,9},{5,13},{9,17},{1... | collective-permute-start | bytes 700424 | tf_op jit(solution)/shard_map/ppermute | solution.py:12
  26.9 17.7 %collective-permute-start.2 = (f32[384,152]{1,0:T(8,128)}, f32[384,152]{1,0:T(8,128)}, u32[]{:S(2)}, u32[]{:S(2)}) collective-permute-start(f32[384,152]{1,0:T(8,128)} %gather_fusion.3), channel_id=1, source_target_pairs={{4,0},{8,4},{12,8},{16,12},{20,16},{24,20},{28,24},{5,1},{9,5},{13... | collective-permute-start | bytes 700424 | tf_op jit(solution)/shard_map/ppermute | solution.py:12
  28.2 15.3 %copy-start.1 = (s32[1024,79]{0,1:T(8,128)S(1)}, s32[1024,79]{0,1:T(8,128)}, u32[]{:S(2)}) copy-start(s32[1024,79]{0,1:T(8,128)} %param.10) | copy-start | bytes 970756
  47.3 418.6 %copy-start.2 = (f32[256,152]{0,1:T(8,128)S(1)}, f32[256,152]{0,1:T(8,128)}, u32[]{:S(2)}) copy-start(f32[256,152]{0,1:T(8,128)} %param.8) | copy-start | bytes 466948
Sparse Core Ops, SparseCore 0:
  442.2 23.6 reduce-scatter.1
where the time goes:
time: 477 us; the launch traced here: 474 us
  local copies, waits for them, and re-layouts  352 us (74%)
  matrix products  65.9 us (14%)
  waiting for transfers between devices  23.8 us (5%)
  between operations  13.6 us (3%)
  starting transfers between devices  12 us (3%)
  other arithmetic  6.45 us (1%)
    gather x6, local copies, waits for them, and re-layouts, one_block(): picked = jnp.take(lookup, index_block.reshape(-1), axis=0)  305 us
    dot_general x2, matrix products, one_block(): jnp.dot(picked.reshape(block_rows, -1), flat_ops, precision=lax.Precision...  65.9 us
    reduce_scatter x1, waiting for transfers between devices, local(): lax.psum_scatter(partial_value, 'sub', scatter_dimension=0, tiled=True)  23.8 us
    unnamed x9, local copies, waits for them, and re-layouts  18.7 us
    dynamic_update_slice x4, local copies, waits for them, and re-layouts, local(): lax.scan(one_block, jnp.zeros((), jnp.float32), safe_index.reshape(block_...  14.2 us
    ppermute x4, starting transfers between devices, passed_along(): return lax.ppermute(block, axis, route)  12 us
  transfers between devices with their start and end apart: 5, of which 1 were waited for; matrix products, arithmetic and copies ran while one was open for 5% of the time, Pallas kernels for 0%

commit v1 on v0

v1 whole, which is shorter than its diff:
```python
import functools

import jax
import jax.numpy as jnp
from jax import lax
from jax.experimental import pallas as pl
from jax.experimental.pallas import tpu as pltpu
from jax.sharding import PartitionSpec as P

LANES = 128


def passed_along(block, axis, distance):
    devices = range(lax.axis_size(axis))
    route = [(i - distance, i) for i in devices if i - distance in devices]
    return lax.ppermute(block, axis, route)


def translate(width, rows, ids, prev_op, this_op, table, out, odd, even):
    tail = width - LANES
    step = pl.program_id(0)

    @pl.when(step == 0)
    def _():
        out[...] = jnp.zeros_like(out)
        odd[...] = jnp.zeros_like(odd)

    def gather(half, target):
        for r in range(rows):
            target[r] = table[ids[0, 0, half * rows + r]]

    def weights(op):
        full = op[0]
        high = full.astype(jnp.bfloat16).astype(jnp.float32)
        low = full - high
        pad = jnp.zeros((LANES // 4 - tail, width), jnp.float32)
        end = jnp.zeros((LANES // 4, width), jnp.float32)
        mix = jnp.concatenate(
            [high[LANES:], pad, high[LANES:], pad, low[LANES:], pad, end], axis=0
        )
        first = high[:LANES].astype(jnp.bfloat16)
        second = low[:LANES].astype(jnp.bfloat16)
        return (
            jnp.concatenate([first, first], axis=0),
            jnp.concatenate([second, mix.astype(jnp.bfloat16)], axis=0),
        )

    def product(op, source):
        flat = source.reshape(2 * rows, LANES)
        head = flat[pl.ds(0, rows, stride=2), :]
        rest = flat[pl.ds(1, rows, stride=2), :]
        head_high = head.astype(jnp.bfloat16)
        head_low = (head - head_high.astype(jnp.float32)).astype(jnp.bfloat16)
        rest_high = rest.astype(jnp.bfloat16).astype(jnp.float32)
        lane = lax.broadcasted_iota(jnp.int32, rest.shape, 1)
        second = (lane >= LANES // 4) & (lane < LANES // 2)
        rest_mix = jnp.where(second, rest - rest_high, rest_high).astype(jnp.bfloat16)
        first_w, second_w = weights(op)
        out[...] += jnp.dot(
            jnp.concatenate([head_high, head_low], axis=1),
            first_w,
            preferred_element_type=jnp.float32,
        ) + jnp.dot(
            jnp.concatenate([head_high, rest_mix], axis=1),
            second_w,
            preferred_element_type=jnp.float32,
        )

    gather(0, even)
    product(prev_op, odd)
    gather(1, odd)
    product(this_op, even)


def partial_sum(table, ids, operators, rows):
    count, width, _ = operators.shape
    steps = ids.shape[0]
    return pl.pallas_call(
        functools.partial(translate, width, rows),
        grid=(steps,),
        in_specs=[
            pl.BlockSpec((1, 1, 2 * rows), lambda i: (i, 0, 0), memory_space=pltpu.SMEM),
            pl.BlockSpec((1, width, width), lambda i: (jnp.maximum(2 * i - 1, 0), 0, 0)),
            pl.BlockSpec((1, width, width), lambda i: (jnp.minimum(2 * i, count - 1), 0, 0)),
            pl.BlockSpec(memory_space=pltpu.VMEM),
        ],
        out_specs=pl.BlockSpec((rows, width), lambda i: (0, 0)),
        out_shape=jax.ShapeDtypeStruct((rows, width), jnp.float32),
        scratch_shapes=[
            pltpu.VMEM((rows, 2, LANES), jnp.float32),
            pltpu.VMEM((rows, 2, LANES), jnp.float32),
        ],
        compiler_params=pltpu.CompilerParams(
            dimension_semantics=("arbitrary",), vmem_limit_bytes=48 * 1024 * 1024
        ),
    )(ids, operators, operators, table)


def local(multipole, inherited, send_rows, sources, operators):
    near_count = send_rows.shape[1] // 2
    rows, width = multipole.shape
    count = operators.shape[0]
    tail = width - LANES
    gap = jnp.zeros((rows, LANES // 4 - tail), jnp.float32)
    end = multipole[:, LANES:]
    wide = jnp.concatenate(
        [multipole[:, :LANES], end, gap, end, gap, end, gap, jnp.zeros((rows, LANES // 4), jnp.float32)], axis=1
    )
    send_map = send_rows[0]
    payloads = [wide]
    for peer_slot in range(2 * near_count):
        offset = peer_slot + 1 if peer_slot < near_count else near_count - 1 - peer_slot
        payloads.append(passed_along(wide[send_map[peer_slot]], "space", offset))
    payloads.append(jnp.zeros((8, 2 * LANES), jnp.float32))
    table = jnp.concatenate(payloads, axis=0)
    empty_row = table.shape[0] - 8
    table = table.reshape(-1, 2, LANES)

    steps = count // 2 + 1
    safe = jnp.where(sources >= 0, sources, empty_row)
    safe = jnp.pad(safe, ((0, 0), (0, 2 * steps - count)), constant_values=empty_row)
    ids = safe.T.reshape(steps, 1, 2 * rows)
    total = partial_sum(table, ids, operators, rows)
    summed = lax.psum_scatter(total, "sub", scatter_dimension=0, tiled=True)
    return summed + inherited


def solution(mesh):
    return jax.shard_map(
        local,
        mesh=mesh,
        in_specs=(
            P("space", None),
            P(("space", "sub"), None),
            P("space", None, None),
            P("space", "sub"),
            P("sub", None, None),
        ),
        out_specs=P(("space", "sub"), None),
        check_vma=False,
    )
```

time: 477 us -> 204 us (0.43)
  local copies, waits for them, and re-layouts: 352 us -> 40.6 us
  Pallas kernels: 0 us -> 106 us
  matrix products: 65.9 us -> 0 us
  waiting for transfers between devices: 23.8 us -> 29.1 us
    gather x10 -> x4, local copies, waits for them, and re-layouts: 312 us -> 6.68 us  [local(): payloads.append(passed_along(wide[send_map[peer_slot]], 'space', offset))]
    pallas_call x0 -> x1, Pallas kernels: none -> 106 us  [partial_sum(): pl.pallas_call(functools.partial(translate, width, rows), grid=(steps,),...]
    dot_general x2 -> x0, matrix products: 65.9 us -> none  [one_block(): jnp.dot(picked.reshape(block_rows, -1), flat_ops, precision=lax.Precision...]
    dynamic_update_slice x4 -> x0, local copies, waits for them, and re-layouts: 14.2 us -> none  [local(): lax.scan(one_block, jnp.zeros((), jnp.float32), safe_index.reshape(block_...]
    unnamed x9 -> x14, local copies, waits for them, and re-layouts: 18.7 us -> 24 us
    reduce_scatter x1, waiting for transfers between devices: 23.8 us -> 29.1 us  [local(): summed = lax.psum_scatter(total, 'sub', scatter_dimension=0, tiled=True)]
  transfers between devices with their start and end apart: 5 -> 5, of which waited for: 1 -> 1; matrix products, arithmetic and copies ran while one was open for 5% -> 13% of each run, Pallas kernels for 0% -> 0%
where the time goes in v1:
time: 204 us; the launch traced here: 203 us
  Pallas kernels  106 us (52%)
  local copies, waits for them, and re-layouts  40.6 us (20%)
  waiting for transfers between devices  29.1 us (14%)
  between operations  13.6 us (7%)
  starting transfers between devices  10.9 us (5%)
  other arithmetic  2.05 us (1%)
    pallas_call x1, Pallas kernels, partial_sum(): pl.pallas_call(functools.partial(translate, width, rows), grid=(steps,),...  106 us
    reduce_scatter x1, waiting for transfers between devices, local(): summed = lax.psum_scatter(total, 'sub', scatter_dimension=0, tiled=True)  29.1 us
    unnamed x14, local copies, waits for them, and re-layouts  24 us
    ppermute x4, starting transfers between devices, passed_along(): return lax.ppermute(block, axis, route)  10.9 us
    gather x4, local copies, waits for them, and re-layouts, local(): payloads.append(passed_along(wide[send_map[peer_slot]], 'space', offset))  6.68 us
    concatenate x1, local copies, waits for them, and re-layouts, local(): jnp.concatenate([multipole[:, :LANES], end, gap, end, gap, end, gap, jnp....  4.17 us
  transfers between devices with their start and end apart: 5, of which 1 were waited for; matrix products, arithmetic and copies ran while one was open for 13% of the time, Pallas kernels for 0%

profile of v1, /device:TPU:0, one launch (start us, length us, event | category | flops | bytes accessed | tf_op | source)
XLA Modules:
  0.0 202.8 jit_solution(5163571410946165269)
XLA Ops:
  6.5 1.4 copy.19
  8.1 0.8 broadcast_in_dim.19
  8.9 4.2 %concatenate.7 = f32[1024,256]{1,0:T(8,128)S(1)} concatenate(f32[1024,152]{1,0:T(8,128)S(1)} %copy.19, f32[1024,8]{1,0:T(8,128)S(1)} %broadcast_in_dim.18, f32[1024,24]{1,0:T(8,128)S(1)} %slice.34, f32[1024,8]{1,0:T(8,128)S(1)} %broadcast_in_dim.18, f32[1024,24]{1,0:T(8,128)S(1)} %slice.34, f32[1024,8]{1,0:T(8,128)S(1)} %broadcast_in_dim.18, f32[1024,32]{1,0:T(8,128)} %broadcast_in_dim.19), dimensions={1} | concatenate | bytes 2097152 | tf_op jit(solution)/shard_map/concatenate | solution.py:106
  13.1 1.7 gather_fusion
  14.8 4.9 %collective-permute-start = (f32[384,256]{1,0:T(8,128)S(1)}, f32[384,256]{1,0:T(8,128)S(1)}, u32[]{:S(2)}, u32[]{:S(2)}) collective-permute-start(f32[384,256]{1,0:T(8,128)S(1)} %gather_fusion), channel_id=1, source_target_pairs={{0,4},{4,8},{8,12},{12,16},{16,20},{20,24},{24,28},{1,5},{5,9},{9,... | collective-permute-start | bytes 1179656 | tf_op jit(solution)/shard_map/ppermute | solution.py:16
  19.7 1.7 gather_fusion.1
  21.4 3.5 %collective-permute-start.1 = (f32[384,256]{1,0:T(8,128)S(1)}, f32[384,256]{1,0:T(8,128)S(1)}, u32[]{:S(2)}, u32[]{:S(2)}) collective-permute-start(f32[384,256]{1,0:T(8,128)S(1)} %gather_fusion.1), channel_id=1, source_target_pairs={{0,8},{4,12},{8,16},{12,20},{16,24},{20,28},{1,9},{5,13},{9,17},{1... | collective-permute-start | bytes 1179656 | tf_op jit(solution)/shard_map/ppermute | solution.py:16
  24.9 1.7 gather_fusion.2
  26.5 1.3 collective-permute-start.2
  27.9 1.7 gather_fusion.3
  29.5 1.3 collective-permute-start.3
  30.8 1.0 compare_select_fusion
  31.8 1.1 constant_dynamic-update-slice_fusion.5
  33.0 15.3 %copy.20.prev_op.this_op = f32[79,152,152]{2,1,0:T(8,128)} copy(f32[79,152,152]{0,2,1:T(8,128)} %param.9) | data formatting | bytes 14601728 | tf_op args[4]
  48.3 0.4 reshape.126.ids
  48.6 0.0 collective-permute-done
  48.6 0.8 constant_dynamic-update-slice_fusion.4
  49.4 0.0 collective-permute-done.1
  49.4 0.8 constant_dynamic-update-slice_fusion.3
  50.2 1.8 constant_dynamic-update-slice_fusion.2
  52.0 0.0 collective-permute-done.3
  52.0 1.8 constant_dynamic-update-slice_fusion.1
  53.7 0.6 constant_dynamic-update-slice_fusion
  54.3 3.1 %reshape.127.table = f32[2568,2,128]{2,1,0:T(2,128)S(1)} reshape(f32[2568,256]{1,0:T(8,128)} %constant_dynamic-update-slice_fusion) | data formatting | bytes 5259264 | tf_op jit(solution)/shard_map/reshape | solution.py:117
  57.4 0.0 copy-start.1
  57.4 106.5 %shard_map.55 = f32[1024,152]{1,0:T(8,128)S(1)} custom-call(s32[40,1,2048]{2,1,0:T(1,128)S(1)} %reshape.126.ids, f32[79,152,152]{2,1,0:T(8,128)} %copy.20.prev_op.this_op, f32[79,152,152]{2,1,0:T(8,128)} %copy.20.prev_op.this_op, f32[2568,2,128]{2,1,0:T(2,128)S(1)} %reshape.127.table), custom_call_target="tpu_custom_call" | custom-call | tf_op jit(solution)/shard_map/pallas_call | solution.py:78
  163.9 1.0 copy-done
  164.9 0.0 reduce-scatter.2.cloned.1.call-update
  164.9 0.1 copy.22
  165.1 29.1 %reduce-scatter.2.cloned.1.call-done = f32[256,152]{1,0:T(8,128)} async-done(((f32[1024,152]{1,0:T(8,128)}), f32[256,152]{1,0:T(8,128)}) %reduce-scatter.2.cloned.1.call-update) | async-done | bytes 155664 | tf_op jit(solution)/shard_map/reduce_scatter | solution.py:124
  194.2 1.0 add.51
  195.1 0.8 copy.23
  (14 shorter events, 0.2 us)
Async XLA Ops:
  6.5 1.5 copy-start.2
  6.5 187.6 %reduce-scatter.2.cloned.1.call-start = ((), (), s32[]{:S(2)}) async-start(), calls=%async_computation.1 | async-start | bytes 1310720 | tf_op jit(solution)/shard_map/reduce_scatter | solution.py:124
  14.8 33.8 %collective-permute-start = (f32[384,256]{1,0:T(8,128)S(1)}, f32[384,256]{1,0:T(8,128)S(1)}, u32[]{:S(2)}, u32[]{:S(2)}) collective-permute-start(f32[384,256]{1,0:T(8,128)S(1)} %gather_fusion), channel_id=1, source_target_pairs={{0,4},{4,8},{8,12},{12,16},{16,20},{20,24},{24,28},{1,5},{5,9},{9,... | collective-permute-start | bytes 1179656 | tf_op jit(solution)/shard_map/ppermute | solution.py:16
  21.4 28.1 %collective-permute-start.1 = (f32[384,256]{1,0:T(8,128)S(1)}, f32[384,256]{1,0:T(8,128)S(1)}, u32[]{:S(2)}, u32[]{:S(2)}) collective-permute-start(f32[384,256]{1,0:T(8,128)S(1)} %gather_fusion.1), channel_id=1, source_target_pairs={{0,8},{4,12},{8,16},{12,20},{16,24},{20,28},{1,9},{5,13},{9,17},{1... | collective-permute-start | bytes 1179656 | tf_op jit(solution)/shard_map/ppermute | solution.py:16
  26.5 23.7 %collective-permute-start.2 = (f32[384,256]{1,0:T(8,128)S(1)}, f32[384,256]{1,0:T(8,128)}, u32[]{:S(2)}, u32[]{:S(2)}) collective-permute-start(f32[384,256]{1,0:T(8,128)S(1)} %gather_fusion.2), channel_id=1, source_target_pairs={{4,0},{8,4},{12,8},{16,12},{20,16},{24,20},{28,24},{5,1},{9,5},{13... | collective-permute-start | bytes 1179656 | tf_op jit(solution)/shard_map/ppermute | solution.py:16
  29.5 22.4 %collective-permute-start.3 = (f32[384,256]{1,0:T(8,128)S(1)}, f32[384,256]{1,0:T(8,128)}, u32[]{:S(2)}, u32[]{:S(2)}) collective-permute-start(f32[384,256]{1,0:T(8,128)S(1)} %gather_fusion.3), channel_id=1, source_target_pairs={{8,0},{12,4},{16,8},{20,12},{24,16},{28,20},{9,1},{13,5},{17,9},{2... | collective-permute-start | bytes 1179656 | tf_op jit(solution)/shard_map/ppermute | solution.py:16
  57.4 107.5 %copy-start.1 = (f32[256,152]{0,1:T(8,128)S(1)}, f32[256,152]{0,1:T(8,128)}, u32[]{:S(2)}) copy-start(f32[256,152]{0,1:T(8,128)} %param.6) | copy-start | bytes 466948
  163.9 1.0 copy-start
Sparse Core Ops, SparseCore 0:
  165.1 29.0 reduce-scatter.1

commit v2 on v1

v2 whole, which is shorter than its diff:
```python
import functools

import jax
import jax.numpy as jnp
from jax import lax
from jax.experimental import pallas as pl
from jax.experimental.pallas import tpu as pltpu
from jax.sharding import PartitionSpec as P

LANES = 128


def passed_along(block, axis, distance):
    devices = range(lax.axis_size(axis))
    route = [(i - distance, i) for i in devices if i - distance in devices]
    return lax.ppermute(block, axis, route)


def translate(width, rows, ids, op, block, *refs):
    ghosts, (out, table, odd, even) = refs[:-4], refs[-4:]
    tail = width - LANES
    step = pl.program_id(0)
    flat_table = table.reshape(2 * table.shape[0], LANES)

    def widen(part, start):
        count = part.shape[0]
        flat_table[pl.ds(2 * start, count, stride=2), :] = part[:, :LANES]
        rest = jnp.concatenate(
            [part[:, LANES:], jnp.zeros((count, LANES - tail), jnp.float32)], axis=1
        )
        spread = rest + pltpu.roll(rest, LANES // 4, 1) + pltpu.roll(rest, LANES // 2, 1)
        flat_table[pl.ds(2 * start + 1, count, stride=2), :] = spread

    @pl.when(step == 0)
    def _():
        out[...] = jnp.zeros_like(out)
        odd[...] = jnp.zeros_like(odd)
        start = 0
        for part in (block, *ghosts):
            widen(part, start)
            start += part.shape[0]
        flat_table[2 * start :, :] = jnp.zeros((2 * (table.shape[0] - start), LANES), jnp.float32)

    def gather(half, target):
        for r in range(rows):
            target[r] = table[ids[0, 0, half * rows + r]]

    def weights(index):
        full = op[index]
        high = full.astype(jnp.bfloat16).astype(jnp.float32)
        low = full - high
        pad = jnp.zeros((LANES // 4 - tail, width), jnp.float32)
        end = jnp.zeros((LANES // 4, width), jnp.float32)
        mix = jnp.concatenate(
            [high[LANES:], pad, high[LANES:], pad, low[LANES:], pad, end], axis=0
        )
        first = high[:LANES].astype(jnp.bfloat16)
        second = low[:LANES].astype(jnp.bfloat16)
        return jnp.concatenate([first, first, second, mix.astype(jnp.bfloat16)], axis=0)

    def product(index, source):
        flat = source.reshape(2 * rows, LANES)
        head = flat[pl.ds(0, rows, stride=2), :]
        rest = flat[pl.ds(1, rows, stride=2), :]
        head_high = head.astype(jnp.bfloat16)
        head_low = (head - head_high.astype(jnp.float32)).astype(jnp.bfloat16)
        rest_high = rest.astype(jnp.bfloat16).astype(jnp.float32)
        lane = lax.broadcasted_iota(jnp.int32, rest.shape, 1)
        second = (lane >= LANES // 4) & (lane < LANES // 2)
        rest_mix = jnp.where(second, rest - rest_high, rest_high).astype(jnp.bfloat16)
        out[...] += jnp.dot(
            jnp.concatenate([head_high, head_low, head_high, rest_mix], axis=1),
            weights(index),
            preferred_element_type=jnp.float32,
        )

    gather(0, even)
    product(jnp.maximum(2 * step - 1, 0), odd)
    gather(1, odd)
    product(jnp.minimum(2 * step, op.shape[0] - 1), even)


def partial_sum(block, ghosts, ids, operators):
    rows, width = block.shape
    steps = ids.shape[0]
    table_rows = rows + sum(g.shape[0] for g in ghosts) + 8
    whole = pl.BlockSpec(memory_space=pltpu.VMEM)
    return pl.pallas_call(
        functools.partial(translate, width, rows),
        grid=(steps,),
        in_specs=[
            pl.BlockSpec((1, 1, 2 * rows), lambda i: (i, 0, 0), memory_space=pltpu.SMEM),
        ]
        + [whole] * (2 + len(ghosts)),
        out_specs=pl.BlockSpec((rows, width), lambda i: (0, 0)),
        out_shape=jax.ShapeDtypeStruct((rows, width), jnp.float32),
        scratch_shapes=[
            pltpu.VMEM((table_rows, 2, LANES), jnp.float32),
            pltpu.VMEM((rows, 2, LANES), jnp.float32),
            pltpu.VMEM((rows, 2, LANES), jnp.float32),
        ],
        compiler_params=pltpu.CompilerParams(
            dimension_semantics=("arbitrary",), vmem_limit_bytes=48 * 1024 * 1024
        ),
    )(ids, operators, block, *ghosts)


def reduce_scatter(n, total, inherited, out, outgoing, incoming, send_sems, recv_sems):
    space, me = lax.axis_index("space"), lax.axis_index("sub")
    chunk = out.shape[1]
    peers = [lax.rem(me + k, n) for k in range(1, n)]
    barrier = pltpu.get_barrier_semaphore()
    for peer in peers:
        pl.semaphore_signal(
            barrier, inc=1, device_id=(space, peer), device_id_type=pl.DeviceIdType.MESH
        )
    pl.semaphore_wait(barrier, n - 1)
    copies = []
    for k, peer in enumerate(peers):
        outgoing[k] = total[pl.ds(pl.multiple_of(peer * chunk, chunk), chunk), :].T
        copy = pltpu.make_async_remote_copy(
            src_ref=outgoing.at[k],
            dst_ref=incoming.at[k],
            send_sem=send_sems.at[k],
            recv_sem=recv_sems.at[k],
            device_id=(space, peer),
            device_id_type=pl.DeviceIdType.MESH,
        )
        copy.start()
        copies.append(copy)
    out[...] = inherited[...] + total[pl.ds(pl.multiple_of(me * chunk, chunk), chunk), :].T
    for k, copy in enumerate(copies):
        copy.wait()
        out[...] += incoming[k]


def scatter_sum(total, inherited, n):
    width, chunk = inherited.shape
    whole = pl.BlockSpec(memory_space=pltpu.VMEM)
    return pl.pallas_call(
        functools.partial(reduce_scatter, n),
        in_specs=[whole] * 2,
        out_specs=whole,
        out_shape=jax.ShapeDtypeStruct((width, chunk), jnp.float32),
        scratch_shapes=[
            pltpu.VMEM((n - 1, width, chunk), jnp.float32),
            pltpu.VMEM((n - 1, width, chunk), jnp.float32),
            pltpu.SemaphoreType.DMA((n - 1,)),
            pltpu.SemaphoreType.DMA((n - 1,)),
        ],
        compiler_params=pltpu.CompilerParams(collective_id=0, has_side_effects=True),
    )(total, inherited)


def local(multipole, inherited, send_rows, sources, operators):
    near_count = send_rows.shape[1] // 2
    rows = multipole.shape[0]
    count = operators.shape[0]
    send_map = send_rows[0]
    picked = multipole[send_map.reshape(-1)].reshape(*send_map.shape, -1)
    ghosts = []
    for peer_slot in range(2 * near_count):
        offset = peer_slot + 1 if peer_slot < near_count else near_count - 1 - peer_slot
        ghosts.append(passed_along(picked[peer_slot], "space", offset))
    empty_row = rows + send_map.size
    steps = count // 2 + 1
    safe = jnp.where(sources >= 0, sources, empty_row)
    safe = jnp.pad(safe, ((0, 0), (0, 2 * steps - count)), constant_values=empty_row)
    ids = safe.T.reshape(steps, 1, 2 * rows)
    total = partial_sum(multipole, ghosts, ids, operators)
    return scatter_sum(total, inherited.T, lax.axis_size("sub")).T


def solution(mesh):
    return jax.shard_map(
        local,
        mesh=mesh,
        in_specs=(
            P("space", None),
            P(("space", "sub"), None),
            P("space", None, None),
            P("space", "sub"),
            P("sub", None, None),
        ),
        out_specs=P(("space", "sub"), None),
        check_vma=False,
    )
```

time: 204 us -> 152 us (0.75)
  waiting for transfers between devices: 29.1 us -> 0.75 us
  local copies, waits for them, and re-layouts: 40.6 us -> 25.3 us
  between operations: 13.6 us -> 0.13 us
  Pallas kernels: 106 us -> 112 us
    reduce_scatter x1 -> x0, waiting for transfers between devices: 29.1 us -> none  [local(): summed = lax.psum_scatter(total, 'sub', scatter_dimension=0, tiled=True)]
    pallas_call x0 -> x1, Pallas kernels: none -> 10.9 us  [scatter_sum(): pl.pallas_call(functools.partial(reduce_scatter, n), in_specs=[whole] * 2...]
    pallas_call x1, Pallas kernels: 106 us -> 101 us  [partial_sum(): pl.pallas_call(functools.partial(translate, width, rows), grid=(steps,),...]
    concatenate x2 -> x0, local copies, waits for them, and re-layouts: 4.76 us -> none  [the longest x1 4.17 us: local(): jnp.concatenate([multipole[:, :LANES], end, gap, end, gap, end, gap, jnp....]
    unnamed x14 -> x8, local copies, waits for them, and re-layouts: 24 us -> 19.9 us
    reshape x1 -> x0, local copies, waits for them, and re-layouts: 3.09 us -> none  [local(): table = table.reshape(-1, 2, LANES)]
    gather x4 -> x1, local copies, waits for them, and re-layouts: 6.68 us -> 3.66 us  [local(): picked = multipole[send_map.reshape(-1)].reshape(*send_map.shape, -1)]
  transfers between devices with their start and end apart: 5 -> 4, of which waited for: 1 -> 1; matrix products, arithmetic and copies ran while one was open for 13% -> 10% of each run, Pallas kernels for 0% -> 0%
where the time goes in v2:
time: 152 us; the launch traced here: 151 us
  Pallas kernels  112 us (74%)
  local copies, waits for them, and re-layouts  25.3 us (17%)
  starting transfers between devices  12.7 us (8%)
    pallas_call x1, Pallas kernels, partial_sum(): pl.pallas_call(functools.partial(translate, width, rows), grid=(steps,),...  101 us
    unnamed x8, local copies, waits for them, and re-layouts  19.9 us
    ppermute x4, starting transfers between devices, passed_along(): return lax.ppermute(block, axis, route)  12.7 us
    pallas_call x1, Pallas kernels, scatter_sum(): pl.pallas_call(functools.partial(reduce_scatter, n), in_specs=[whole] * 2...  10.9 us
    gather x1, local copies, waits for them, and re-layouts, local(): picked = multipole[send_map.reshape(-1)].reshape(*send_map.shape, -1)  3.66 us
  transfers between devices with their start and end apart: 4, of which 1 were waited for; matrix products, arithmetic and copies ran while one was open for 10% of the time, Pallas kernels for 0%

profile of v2, /device:TPU:0, one launch (start us, length us, event | category | flops | bytes accessed | tf_op | source)
XLA Modules:
  0.0 150.5 jit_solution(7441341835348329716)
XLA Ops:
  0.0 0.7 copy.9
  0.7 1.4 copy.8.block
  2.2 3.7 %gather_fusion = f32[1536,152]{1,0:T(8,128)S(1)} fusion(f32[1024,152]{1,0:T(8,128)S(1)} %copy.8.block, s32[2048]{0:T(1024)S(1)} %pad_clamp_fusion), kind=kCustom, calls=%fused_computation | custom fusion | bytes 1873920 | tf_op jit(solution)/shard_map/gather | solution.py:160
  5.8 0.0 copy-start.1
  5.8 1.3 fusion.1
  7.1 1.3 collective-permute-start.3
  8.4 1.3 collective-permute-start.2
  9.7 6.9 %collective-permute-start.1 = (f32[384,152]{1,0:T(8,128)}, f32[384,152]{1,0:T(8,128)S(1)}, u32[]{:S(2)}, u32[]{:S(2)}) collective-permute-start(f32[384,152]{1,0:T(8,128)} %get-tuple-element.7), channel_id=1, source_target_pairs={{0,8},{4,12},{8,16},{12,20},{16,24},{20,28},{1,9},{5,13},{9,17},{1... | collective-permute-start | bytes 700424 | tf_op jit(solution)/shard_map/ppermute | solution.py:16
  16.6 3.2 %collective-permute-start = (f32[384,152]{1,0:T(8,128)}, f32[384,152]{1,0:T(8,128)S(1)}, u32[]{:S(2)}, u32[]{:S(2)}) collective-permute-start(f32[384,152]{1,0:T(8,128)} %get-tuple-element.8), channel_id=1, source_target_pairs={{0,4},{4,8},{8,12},{12,16},{16,20},{20,24},{24,28},{1,5},{5,9},{9,... | collective-permute-start | bytes 700424 | tf_op jit(solution)/shard_map/ppermute | solution.py:16
  19.9 0.0 copy-done.1
  19.9 0.4 reshape.40.ids
  20.3 15.3 %copy.7.op = f32[79,152,152]{2,1,0:T(8,128)} copy(f32[79,152,152]{0,2,1:T(8,128)} %param.9) | data formatting | bytes 14601728 | tf_op args[4]
  35.6 0.0 collective-permute-done.3.refs_3_
  35.6 0.0 collective-permute-done.2.refs_2_
  35.6 0.0 collective-permute-done.1.refs_1_
  35.6 0.7 collective-permute-done.refs_0_
  36.4 100.7 %shard_map.55.total = f32[1024,152]{1,0:T(8,128)S(1)} custom-call(s32[40,1,2048]{2,1,0:T(1,128)S(1)} %reshape.40.ids, f32[79,152,152]{2,1,0:T(8,128)} %copy.7.op, f32[1024,152]{1,0:T(8,128)S(1)} %copy.8.block, f32[384,152]{1,0:T(8,128)S(1)} %collective-permute-done.refs_0_, f32[384,152]{1,0:T(8,128)S(1)} %collective-permute-done.1.refs_1_, ...), custom_call_target="tpu_custom_call" | custom-call | tf_op jit(solution)/shard_map/pallas_call | solution.py:88
  137.1 0.0 copy-start
  137.1 1.0 copy-done
  138.1 10.9 %shard_map.56 = f32[152,256]{1,0:T(8,128)} custom-call(f32[1024,152]{1,0:T(8,128)} %copy-done, f32[152,256]{1,0:T(8,128)} %bitcast.8), custom_call_target="tpu_custom_call" | custom-call | tf_op jit(solution)/shard_map/pallas_call | solution.py:140
  149.0 1.6 %copy.11 = f32[256,152]{0,1:T(8,128)} copy(f32[256,152]{0,1:T(8,128)} %bitcast.7) | data formatting | bytes 311296
  (4 shorter events, 0.1 us)
Async XLA Ops:
  5.8 14.0 %copy-start.1 = (s32[1024,79]{0,1:T(8,128)S(1)}, s32[1024,79]{0,1:T(8,128)}, u32[]{:S(2)}) copy-start(s32[1024,79]{0,1:T(8,128)} %param.8) | copy-start | bytes 970756
  7.1 28.5 %collective-permute-start.3 = (f32[384,152]{1,0:T(8,128)}, f32[384,152]{1,0:T(8,128)S(1)}, u32[]{:S(2)}, u32[]{:S(2)}) collective-permute-start(f32[384,152]{1,0:T(8,128)} %get-tuple-element.5), channel_id=1, source_target_pairs={{8,0},{12,4},{16,8},{20,12},{24,16},{28,20},{9,1},{13,5},{17,9},{2... | collective-permute-start | bytes 700424 | tf_op jit(solution)/shard_map/ppermute | solution.py:16
  8.4 27.2 %collective-permute-start.2 = (f32[384,152]{1,0:T(8,128)}, f32[384,152]{1,0:T(8,128)S(1)}, u32[]{:S(2)}, u32[]{:S(2)}) collective-permute-start(f32[384,152]{1,0:T(8,128)} %get-tuple-element.6), channel_id=1, source_target_pairs={{4,0},{8,4},{12,8},{16,12},{20,16},{24,20},{28,24},{5,1},{9,5},{13... | collective-permute-start | bytes 700424 | tf_op jit(solution)/shard_map/ppermute | solution.py:16
  9.7 25.9 %collective-permute-start.1 = (f32[384,152]{1,0:T(8,128)}, f32[384,152]{1,0:T(8,128)S(1)}, u32[]{:S(2)}, u32[]{:S(2)}) collective-permute-start(f32[384,152]{1,0:T(8,128)} %get-tuple-element.7), channel_id=1, source_target_pairs={{0,8},{4,12},{8,16},{12,20},{16,24},{20,28},{1,9},{5,13},{9,17},{1... | collective-permute-start | bytes 700424 | tf_op jit(solution)/shard_map/ppermute | solution.py:16
  16.6 19.7 %collective-permute-start = (f32[384,152]{1,0:T(8,128)}, f32[384,152]{1,0:T(8,128)S(1)}, u32[]{:S(2)}, u32[]{:S(2)}) collective-permute-start(f32[384,152]{1,0:T(8,128)} %get-tuple-element.8), channel_id=1, source_target_pairs={{0,4},{4,8},{8,12},{12,16},{16,20},{20,24},{24,28},{1,5},{5,9},{9,... | collective-permute-start | bytes 700424 | tf_op jit(solution)/shard_map/ppermute | solution.py:16
  137.1 1.0 copy-start

commit v3 on v2

--- a/solution.py
+++ b/solution.py
@@ -43,7 +43,7 @@
 
     def gather(half, target):
         for r in range(rows):
-            target[r] = table[ids[0, 0, half * rows + r]]
+            target[r] = flat_table[pl.ds(pl.multiple_of(ids[0, 0, half * rows + r], 2), 2), :]
 
     def weights(index):
         full = op[index]
@@ -166,7 +166,7 @@
     steps = count // 2 + 1
     safe = jnp.where(sources >= 0, sources, empty_row)
     safe = jnp.pad(safe, ((0, 0), (0, 2 * steps - count)), constant_values=empty_row)
-    ids = safe.T.reshape(steps, 1, 2 * rows)
+    ids = (2 * safe).T.reshape(steps, 1, 2 * rows)
     total = partial_sum(multipole, ghosts, ids, operators)
     return scatter_sum(total, inherited.T, lax.axis_size("sub")).T
 

time: 152 us -> 134 us (0.88)
  Pallas kernels: 112 us -> 94.2 us
    pallas_call x1, Pallas kernels: 101 us -> 83.3 us  [partial_sum(): pl.pallas_call(functools.partial(translate, width, rows), grid=(steps,),...]
  transfers between devices with their start and end apart: 4 -> 4, of which waited for: 1 -> 1; matrix products, arithmetic and copies ran while one was open for 10% -> 12% of each run, Pallas kernels for 0% -> 0%
where the time goes in v3:
time: 134 us; the launch traced here: 133 us
  Pallas kernels  94.2 us (70%)
  local copies, waits for them, and re-layouts  25.3 us (19%)
  starting transfers between devices  12.7 us (9%)
    pallas_call x1, Pallas kernels, partial_sum(): pl.pallas_call(functools.partial(translate, width, rows), grid=(steps,),...  83.3 us
    unnamed x8, local copies, waits for them, and re-layouts  19.9 us
    ppermute x4, starting transfers between devices, passed_along(): return lax.ppermute(block, axis, route)  12.7 us
    pallas_call x1, Pallas kernels, scatter_sum(): pl.pallas_call(functools.partial(reduce_scatter, n), in_specs=[whole] * 2...  10.9 us
    gather x1, local copies, waits for them, and re-layouts, local(): picked = multipole[send_map.reshape(-1)].reshape(*send_map.shape, -1)  3.66 us
  transfers between devices with their start and end apart: 4, of which 1 were waited for; matrix products, arithmetic and copies ran while one was open for 12% of the time, Pallas kernels for 0%

profile of v3, /device:TPU:0, one launch (start us, length us, event | category | flops | bytes accessed | tf_op | source)
XLA Modules:
  0.0 133.1 jit_solution(3472776697791245228)
XLA Ops:
  0.0 0.7 copy.9
  0.7 1.4 %copy.8.block = f32[1024,152]{1,0:T(8,128)S(1)} copy(f32[1024,152]{0,1:T(8,128)} %param.5) | data formatting | bytes 1245184 | tf_op args[0]
  2.2 3.7 %gather_fusion = f32[1536,152]{1,0:T(8,128)S(1)} fusion(f32[1024,152]{1,0:T(8,128)S(1)} %copy.8.block, s32[2048]{0:T(1024)S(1)} %pad_clamp_fusion), kind=kCustom, calls=%fused_computation | custom fusion | bytes 1873920 | tf_op jit(solution)/shard_map/gather | solution.py:160
  5.8 0.0 copy-start.1
  5.8 1.3 fusion.1
  7.1 1.3 collective-permute-start.3
  8.4 1.3 collective-permute-start.2
  9.7 6.9 %collective-permute-start.1 = (f32[384,152]{1,0:T(8,128)}, f32[384,152]{1,0:T(8,128)S(1)}, u32[]{:S(2)}, u32[]{:S(2)}) collective-permute-start(f32[384,152]{1,0:T(8,128)} %get-tuple-element.7), channel_id=1, source_target_pairs={{0,8},{4,12},{8,16},{12,20},{16,24},{20,28},{1,9},{5,13},{9,17},{1... | collective-permute-start | bytes 700424 | tf_op jit(solution)/shard_map/ppermute | solution.py:16
  16.6 3.2 %collective-permute-start = (f32[384,152]{1,0:T(8,128)}, f32[384,152]{1,0:T(8,128)S(1)}, u32[]{:S(2)}, u32[]{:S(2)}) collective-permute-start(f32[384,152]{1,0:T(8,128)} %get-tuple-element.8), channel_id=1, source_target_pairs={{0,4},{4,8},{8,12},{12,16},{16,20},{20,24},{24,28},{1,5},{5,9},{9,... | collective-permute-start | bytes 700424 | tf_op jit(solution)/shard_map/ppermute | solution.py:16
  19.9 0.0 copy-done.1
  19.9 0.4 reshape.40.ids
  20.3 15.3 %copy.7.op = f32[79,152,152]{2,1,0:T(8,128)} copy(f32[79,152,152]{0,2,1:T(8,128)} %param.9) | data formatting | bytes 14601728 | tf_op args[4]
  35.6 0.0 collective-permute-done.3.refs_3_
  35.6 0.0 collective-permute-done.2.refs_2_
  35.6 0.0 collective-permute-done.1.refs_1_
  35.6 0.7 collective-permute-done.refs_0_
  36.4 83.3 %shard_map.55.total = f32[1024,152]{1,0:T(8,128)S(1)} custom-call(s32[40,1,2048]{2,1,0:T(1,128)S(1)} %reshape.40.ids, f32[79,152,152]{2,1,0:T(8,128)} %copy.7.op, f32[1024,152]{1,0:T(8,128)S(1)} %copy.8.block, f32[384,152]{1,0:T(8,128)S(1)} %collective-permute-done.refs_0_, f32[384,152]{1,0:T(8,128)S(1)} %collective-permute-done.1.refs_1_, ...), custom_call_target="tpu_custom_call" | custom-call | tf_op jit(solution)/shard_map/pallas_call | solution.py:88
  119.7 0.0 copy-start
  119.7 1.0 copy-done
  120.7 10.9 %shard_map.56 = f32[152,256]{1,0:T(8,128)} custom-call(f32[1024,152]{1,0:T(8,128)} %copy-done, f32[152,256]{1,0:T(8,128)} %bitcast.8), custom_call_target="tpu_custom_call" | custom-call | tf_op jit(solution)/shard_map/pallas_call | solution.py:140
  131.5 1.6 %copy.11 = f32[256,152]{0,1:T(8,128)} copy(f32[256,152]{0,1:T(8,128)} %bitcast.7) | data formatting | bytes 311296
  (4 shorter events, 0.1 us)
Async XLA Ops:
  5.8 14.0 %copy-start.1 = (s32[1024,79]{0,1:T(8,128)S(1)}, s32[1024,79]{0,1:T(8,128)}, u32[]{:S(2)}) copy-start(s32[1024,79]{0,1:T(8,128)} %param.8) | copy-start | bytes 970756
  7.1 28.5 %collective-permute-start.3 = (f32[384,152]{1,0:T(8,128)}, f32[384,152]{1,0:T(8,128)S(1)}, u32[]{:S(2)}, u32[]{:S(2)}) collective-permute-start(f32[384,152]{1,0:T(8,128)} %get-tuple-element.5), channel_id=1, source_target_pairs={{8,0},{12,4},{16,8},{20,12},{24,16},{28,20},{9,1},{13,5},{17,9},{2... | collective-permute-start | bytes 700424 | tf_op jit(solution)/shard_map/ppermute | solution.py:16
  8.4 27.2 %collective-permute-start.2 = (f32[384,152]{1,0:T(8,128)}, f32[384,152]{1,0:T(8,128)S(1)}, u32[]{:S(2)}, u32[]{:S(2)}) collective-permute-start(f32[384,152]{1,0:T(8,128)} %get-tuple-element.6), channel_id=1, source_target_pairs={{4,0},{8,4},{12,8},{16,12},{20,16},{24,20},{28,24},{5,1},{9,5},{13... | collective-permute-start | bytes 700424 | tf_op jit(solution)/shard_map/ppermute | solution.py:16
  9.7 25.9 %collective-permute-start.1 = (f32[384,152]{1,0:T(8,128)}, f32[384,152]{1,0:T(8,128)S(1)}, u32[]{:S(2)}, u32[]{:S(2)}) collective-permute-start(f32[384,152]{1,0:T(8,128)} %get-tuple-element.7), channel_id=1, source_target_pairs={{0,8},{4,12},{8,16},{12,20},{16,24},{20,28},{1,9},{5,13},{9,17},{1... | collective-permute-start | bytes 700424 | tf_op jit(solution)/shard_map/ppermute | solution.py:16
  16.6 19.7 %collective-permute-start = (f32[384,152]{1,0:T(8,128)}, f32[384,152]{1,0:T(8,128)S(1)}, u32[]{:S(2)}, u32[]{:S(2)}) collective-permute-start(f32[384,152]{1,0:T(8,128)} %get-tuple-element.8), channel_id=1, source_target_pairs={{0,4},{4,8},{8,12},{12,16},{16,20},{20,24},{24,28},{1,5},{5,9},{9,... | collective-permute-start | bytes 700424 | tf_op jit(solution)/shard_map/ppermute | solution.py:16
  119.7 1.0 copy-start

commit v4 on v3

--- a/solution.py
+++ b/solution.py
@@ -17,7 +17,9 @@
 
 
 def translate(width, rows, ids, op, block, *refs):
-    ghosts, (out, table, odd, even) = refs[:-4], refs[-4:]
+    ghosts, (out, table, odd, even, op_head, op_rest) = refs[:-6], refs[-6:]
+    count = op.shape[2]
+    stride = op_head.shape[0] // (width + 1)
     tail = width - LANES
     step = pl.program_id(0)
     flat_table = table.reshape(2 * table.shape[0], LANES)
@@ -39,6 +41,14 @@
         for part in (block, *ghosts):
             widen(part, start)
             start += part.shape[0]
+        def turn(i, carry):
+            turned = op[i].T
+            place = pl.ds(pl.multiple_of(i * stride, 8), count)
+            op_head[place, :] = turned[:, :LANES]
+            op_rest[place, :tail] = turned[:, LANES:]
+            return carry
+
+        lax.fori_loop(0, width, turn, 0, unroll=8)
         flat_table[2 * start :, :] = jnp.zeros((2 * (table.shape[0] - start), LANES), jnp.float32)
 
     def gather(half, target):
@@ -46,7 +56,8 @@
             target[r] = flat_table[pl.ds(pl.multiple_of(ids[0, 0, half * rows + r], 2), 2), :]
 
     def weights(index):
-        full = op[index]
+        every = pl.ds(index, width, stride=stride)
+        full = jnp.concatenate([op_head[every, :], op_rest[every, :][:, :tail]], axis=1)
         high = full.astype(jnp.bfloat16).astype(jnp.float32)
         low = full - high
         pad = jnp.zeros((LANES // 4 - tail, width), jnp.float32)
@@ -77,12 +88,13 @@
     gather(0, even)
     product(jnp.maximum(2 * step - 1, 0), odd)
     gather(1, odd)
-    product(jnp.minimum(2 * step, op.shape[0] - 1), even)
+    product(jnp.minimum(2 * step, count - 1), even)
 
 
 def partial_sum(block, ghosts, ids, operators):
     rows, width = block.shape
     steps = ids.shape[0]
+    op_stride = -(-operators.shape[0] // 8) * 8
     table_rows = rows + sum(g.shape[0] for g in ghosts) + 8
     whole = pl.BlockSpec(memory_space=pltpu.VMEM)
     return pl.pallas_call(
@@ -98,11 +110,13 @@
             pltpu.VMEM((table_rows, 2, LANES), jnp.float32),
             pltpu.VMEM((rows, 2, LANES), jnp.float32),
             pltpu.VMEM((rows, 2, LANES), jnp.float32),
+            pltpu.VMEM(((width + 1) * op_stride, LANES), jnp.float32),
+            pltpu.VMEM(((width + 1) * op_stride, LANES), jnp.float32),
         ],
         compiler_params=pltpu.CompilerParams(
             dimension_semantics=("arbitrary",), vmem_limit_bytes=48 * 1024 * 1024
         ),
-    )(ids, operators, block, *ghosts)
+    )(ids, operators.transpose(1, 2, 0), block, *ghosts)
 
 
 def reduce_scatter(n, total, inherited, out, outgoing, incoming, send_sems, recv_sems):

time: 134 us -> 145 us (1.082)
  waiting for transfers between devices: 0.74 us -> 18.8 us
  local copies, waits for them, and re-layouts: 25.3 us -> 9.22 us
  Pallas kernels: 94.2 us -> 105 us
  starting transfers between devices: 12.7 us -> 10.9 us
    ppermute x4, waiting for transfers between devices: 0.74 us -> 18.8 us  [passed_along(): return lax.ppermute(block, axis, route)]
    unnamed x8 -> x9, local copies, waits for them, and re-layouts: 19.9 us -> 3.99 us
    pallas_call x1, Pallas kernels: 83.3 us -> 94 us  [partial_sum(): pl.pallas_call(functools.partial(translate, width, rows), grid=(steps,),...]
    ppermute x4, starting transfers between devices: 12.7 us -> 10.9 us  [passed_along(): return lax.ppermute(block, axis, route)]
  transfers between devices with their start and end apart: 4 -> 4, of which waited for: 1 -> 2; matrix products, arithmetic and copies ran while one was open for 12% -> 0% of each run, Pallas kernels for 0% -> 0%
where the time goes in v4:
time: 145 us; the launch traced here: 144 us
  Pallas kernels  105 us (72%)
  waiting for transfers between devices  18.8 us (13%)
  starting transfers between devices  10.9 us (8%)
  local copies, waits for them, and re-layouts  9.22 us (6%)
    pallas_call x1, Pallas kernels, partial_sum(): pl.pallas_call(functools.partial(translate, width, rows), grid=(steps,),...  94 us
    ppermute x4, waiting for transfers between devices, passed_along(): return lax.ppermute(block, axis, route)  18.8 us
    ppermute x4, starting transfers between devices, passed_along(): return lax.ppermute(block, axis, route)  10.9 us
    pallas_call x1, Pallas kernels, scatter_sum(): pl.pallas_call(functools.partial(reduce_scatter, n), in_specs=[whole] * 2...  10.9 us
    unnamed x9, local copies, waits for them, and re-layouts  3.99 us
    gather x1, local copies, waits for them, and re-layouts, local(): picked = multipole[send_map.reshape(-1)].reshape(*send_map.shape, -1)  3.66 us
  transfers between devices with their start and end apart: 4, of which 2 were waited for; matrix products, arithmetic and copies ran while one was open for 0% of the time, Pallas kernels for 0%

profile of v4, /device:TPU:0, one launch (start us, length us, event | category | flops | bytes accessed | tf_op | source)
XLA Modules:
  0.0 144.0 jit_solution(6295976455814199026)
XLA Ops:
  0.0 0.0 copy-start.2
  0.0 1.4 copy.7.block
  1.4 0.0 copy-done.2
  1.5 3.7 %gather_fusion = f32[1536,152]{1,0:T(8,128)S(1)} fusion(f32[1024,152]{1,0:T(8,128)S(1)} %copy.7.block, s32[2048]{0:T(1024)S(1)} %pad_clamp_fusion), kind=kCustom, calls=%fused_computation | custom fusion | bytes 1873920 | tf_op jit(solution)/shard_map/gather | solution.py:174
  5.2 0.0 copy-start.1
  5.2 1.2 fusion.1
  6.4 4.9 %collective-permute-start = (f32[384,152]{1,0:T(8,128)}, f32[384,152]{1,0:T(8,128)S(1)}, u32[]{:S(2)}, u32[]{:S(2)}) collective-permute-start(f32[384,152]{1,0:T(8,128)} %get-tuple-element.8), channel_id=1, source_target_pairs={{0,4},{4,8},{8,12},{12,16},{16,20},{20,24},{24,28},{1,5},{5,9},{9,... | collective-permute-start | bytes 700424 | tf_op jit(solution)/shard_map/ppermute | solution.py:16
  11.2 3.5 %collective-permute-start.1 = (f32[384,152]{1,0:T(8,128)}, f32[384,152]{1,0:T(8,128)S(1)}, u32[]{:S(2)}, u32[]{:S(2)}) collective-permute-start(f32[384,152]{1,0:T(8,128)} %get-tuple-element.7), channel_id=1, source_target_pairs={{0,8},{4,12},{8,16},{12,20},{16,24},{20,28},{1,9},{5,13},{9,17},{1... | collective-permute-start | bytes 700424 | tf_op jit(solution)/shard_map/ppermute | solution.py:16
  14.7 1.3 collective-permute-start.2
  16.0 1.3 collective-permute-start.3
  17.3 0.0 copy-done.1
  17.4 0.4 reshape.40.ids
  17.8 9.7 %collective-permute-done.refs_0_ = f32[384,152]{1,0:T(8,128)S(1)} collective-permute-done((f32[384,152]{1,0:T(8,128)}, f32[384,152]{1,0:T(8,128)S(1)}, u32[]{:S(2)}, u32[]{:S(2)}) %collective-permute-start) | collective-permute-done | bytes 233504 | tf_op jit(solution)/shard_map/ppermute | solution.py:16
  27.5 0.0 collective-permute-done.1.refs_1_
  27.5 0.0 collective-permute-done.2.refs_2_
  27.5 9.1 %collective-permute-done.3.refs_3_ = f32[384,152]{1,0:T(8,128)S(1)} collective-permute-done((f32[384,152]{1,0:T(8,128)}, f32[384,152]{1,0:T(8,128)S(1)}, u32[]{:S(2)}, u32[]{:S(2)}) %collective-permute-start.3) | collective-permute-done | bytes 233504 | tf_op jit(solution)/shard_map/ppermute | solution.py:16
  36.6 94.0 %shard_map.55.total = f32[1024,152]{1,0:T(8,128)S(1)} custom-call(s32[40,1,2048]{2,1,0:T(1,128)S(1)} %reshape.40.ids, f32[152,152,79]{2,1,0:T(8,128)} %bitcast.8, f32[1024,152]{1,0:T(8,128)S(1)} %copy.7.block, f32[384,152]{1,0:T(8,128)S(1)} %collective-permute-done.refs_0_, f32[384,152]{1,0:T(8,128)S(1)} %collective-permute-done.1.refs_1_, ...), custom_call_target="tpu_custom_call" | custom-call | tf_op jit(solution)/shard_map/pallas_call | solution.py:100
  130.6 0.0 copy-start
  130.6 1.0 copy-done
  131.6 10.9 %shard_map.56 = f32[152,256]{1,0:T(8,128)} custom-call(f32[1024,152]{1,0:T(8,128)} %copy-done, f32[152,256]{1,0:T(8,128)} %bitcast.10), custom_call_target="tpu_custom_call" | custom-call | tf_op jit(solution)/shard_map/pallas_call | solution.py:154
  142.5 1.6 %copy.10 = f32[256,152]{0,1:T(8,128)} copy(f32[256,152]{0,1:T(8,128)} %bitcast.9) | data formatting | bytes 311296
  (5 shorter events, 0.1 us)
Async XLA Ops:
  0.0 1.4 copy-start.2
  5.2 12.2 %copy-start.1 = (s32[1024,79]{0,1:T(8,128)S(1)}, s32[1024,79]{0,1:T(8,128)}, u32[]{:S(2)}) copy-start(s32[1024,79]{0,1:T(8,128)} %param.8) | copy-start | bytes 970756
  6.4 21.1 %collective-permute-start = (f32[384,152]{1,0:T(8,128)}, f32[384,152]{1,0:T(8,128)S(1)}, u32[]{:S(2)}, u32[]{:S(2)}) collective-permute-start(f32[384,152]{1,0:T(8,128)} %get-tuple-element.8), channel_id=1, source_target_pairs={{0,4},{4,8},{8,12},{12,16},{16,20},{20,24},{24,28},{1,5},{5,9},{9,... | collective-permute-start | bytes 700424 | tf_op jit(solution)/shard_map/ppermute | solution.py:16
  11.2 16.3 %collective-permute-start.1 = (f32[384,152]{1,0:T(8,128)}, f32[384,152]{1,0:T(8,128)S(1)}, u32[]{:S(2)}, u32[]{:S(2)}) collective-permute-start(f32[384,152]{1,0:T(8,128)} %get-tuple-element.7), channel_id=1, source_target_pairs={{0,8},{4,12},{8,16},{12,20},{16,24},{20,28},{1,9},{5,13},{9,17},{1... | collective-permute-start | bytes 700424 | tf_op jit(solution)/shard_map/ppermute | solution.py:16
  14.7 12.8 %collective-permute-start.2 = (f32[384,152]{1,0:T(8,128)}, f32[384,152]{1,0:T(8,128)S(1)}, u32[]{:S(2)}, u32[]{:S(2)}) collective-permute-start(f32[384,152]{1,0:T(8,128)} %get-tuple-element.6), channel_id=1, source_target_pairs={{4,0},{8,4},{12,8},{16,12},{20,16},{24,20},{28,24},{5,1},{9,5},{13... | collective-permute-start | bytes 700424 | tf_op jit(solution)/shard_map/ppermute | solution.py:16
  16.0 20.6 %collective-permute-start.3 = (f32[384,152]{1,0:T(8,128)}, f32[384,152]{1,0:T(8,128)S(1)}, u32[]{:S(2)}, u32[]{:S(2)}) collective-permute-start(f32[384,152]{1,0:T(8,128)} %get-tuple-element.5), channel_id=1, source_target_pairs={{8,0},{12,4},{16,8},{20,12},{24,16},{28,20},{9,1},{13,5},{17,9},{2... | collective-permute-start | bytes 700424 | tf_op jit(solution)/shard_map/ppermute | solution.py:16
  130.6 1.0 copy-start
